TPU v7x, 32 devices: a whole 2x2x4 slice. The times are simulated.
32 devices in a mesh: row: 4 (over z), col: 4 (over y, x), tm: 2 (over core).
Axes of the slice: x: 2, y: 2, z: 4, core: 2. Of those that a mesh axis runs over, the one named last changes fastest.
Arguments:
- g_occ: float32 [2, 6144, 6144], P('tm', 'row', 'col'), may hold values from -6 to 6
- g_emp: float32 [2, 6144, 6144], P('tm', 'row', 'col'), may hold values from -6 to 6
- basis: float32 [6144, 1024], P('col'), may hold values from -0.078125 to 0.078125
Outputs:
- spectrum: float32 [2, 1024, 1024], P('tm', 'row', 'col')
All inputs are finite; a program needn't handle non-finite values.
Results may differ from a plain program's by a relative error of at most 0.000071.
Values sent between devices are 32-bit elements; how exact they have to be, the bound alone decides.
No kernel may reach another device: no remote copies, remote signals or barrier semaphores. Data moves between devices by JAX's collectives and lax.ppermute only.
A program may use at most 128 MiB of HBM per device.

v0:
```python
import jax
import jax.numpy as jnp
from jax import lax
from jax.sharding import PartitionSpec as P

HIGHEST_PRECISION = lax.Precision.HIGHEST


def broadcast(block, axis, source):
    block = jnp.where(lax.axis_index(axis) == source, block, jnp.zeros_like(block))
    return lax.psum(block, axis)


def per_device(g_occ, g_emp, basis):
    response = g_occ[0] * g_emp[0]
    rows_dev = response.shape[0]
    cols_dev = basis.shape[0]
    first_row = lax.axis_index("row") * rows_dev
    owner = first_row // cols_dev
    offset_local = first_row % cols_dev
    mine = lax.dynamic_slice_in_dim(basis, offset_local, rows_dev, 0)
    panel = broadcast(mine, "col", owner)
    mixed = jnp.dot(
        response, basis, precision=HIGHEST_PRECISION, preferred_element_type=jnp.float32
    )
    mixed_rows = lax.psum_scatter(mixed, "col", scatter_dimension=1, tiled=True)
    projected = lax.psum_scatter(
        lax.dot_general(
            panel,
            mixed_rows,
            (((0,), (0,)), ((), ())),
            precision=HIGHEST_PRECISION,
            preferred_element_type=jnp.float32,
        ),
        "row",
        scatter_dimension=0,
        tiled=True,
    )
    points = lax.axis_size("tm")
    moment = lax.axis_index("tm").astype(jnp.float32)
    orders = jnp.arange(1 * lax.axis_size("tm"), dtype=jnp.int32).astype(jnp.float32)
    weights = jnp.sqrt(2.0 / points) * jnp.cos(jnp.pi * (orders + 0.5) * (moment + 0.5) / points)
    return lax.psum_scatter(
        weights[:, None, None] * projected[None, :, :], "tm", scatter_dimension=0, tiled=True
    )


def solution(mesh):
    return jax.shard_map(
        per_device,
        mesh=mesh,
        in_specs=(P("tm", "row", "col"), P("tm", "row", "col"), P("col", None)),
        out_specs=P("tm", "row", "col"),
        check_vma=False,
    )
```

profile of v0, /device:TPU:0, one launch (start us, length us, event | category | flops | bytes accessed | tf_op | source)
XLA Modules:
  0.0 283.3 jit_solution(11242491472990814980)
XLA Ops:
  6.5 0.0 all-reduce.2.cloned.1.call-start
  6.5 6.8 %broadcast_select_fusion = f32[1536,1024]{1,0:T(8,128)} fusion(f32[1536,1024]{1,0:T(8,128)} %param.5, pred[]{:T(512)S(6)} %eq.5), kind=kLoop, calls=%fused_computation.3 | loop fusion | flops 1572864 | bytes 12582913 | tf_op jit(solution)/shard_map/jit(_where)/select_n | solution.py:10
  13.4 0.0 all-reduce.2.cloned.1.call-update
  13.4 0.0 reduce-scatter.4.cloned.1.call-start
  13.4 36.6 %fusion = f32[1536,1024]{1,0:T(8,128)} fusion(f32[1536,1024]{1,0:T(8,128)} %param.5, f32[1,1536,1536]{2,1,0:T(8,128)} %param.3, f32[1,1536,1536]{2,1,0:T(8,128)} %param.4), kind=kOutput, calls=%fused_computation | convolution fusion | flops 28993388544 | bytes 31457280 | tf_op jit(solution)/shard_map/dot_general | solution.py:23
  50.1 0.0 reduce-scatter.4.cloned.1.call-update
  50.1 0.2 reduce-scatter.6.cloned.1.call-start
  50.3 104.1 %all-reduce.2.cloned.1.call-done = f32[1536,1024]{1,0:T(8,128)} async-done(((f32[1536,1024]{1,0:T(8,128)}), f32[1536,1024]{1,0:T(8,128)}) %all-reduce.2.cloned.1.call-update) | async-done | bytes 6291472 | tf_op jit(solution)/shard_map/psum | solution.py:11
  154.4 73.1 %reduce-scatter.4.cloned.1.call-done = f32[1536,256]{1,0:T(8,128)} async-done(((f32[1536,1024]{1,0:T(8,128)}), f32[1536,256]{1,0:T(8,128)}) %reduce-scatter.4.cloned.1.call-update) | async-done | bytes 1572880 | tf_op jit(solution)/shard_map/reduce_scatter | solution.py:26
  227.5 13.3 %fusion.3 = f32[1024,256]{1,0:T(8,128)} fusion(f32[1536,1024]{1,0:T(8,128)} %all-reduce.2.cloned.1.call-done, f32[1536,256]{1,0:T(8,128)} %reduce-scatter.4.cloned.1.call-done), kind=kOutput, calls=%fused_computation.6 | convolution fusion | flops 4831838208 | bytes 8912896 | tf_op jit(solution)/shard_map/dot_general | solution.py:28
  240.7 0.0 reduce-scatter.6.cloned.1.call-update
  240.8 0.0 reduce-scatter.8.cloned.1.call-start
  240.9 27.3 %reduce-scatter.6.cloned.1.call-done = f32[256,256]{1,0:T(8,128)} async-done(((f32[1024,256]{1,0:T(8,128)}), f32[256,256]{1,0:T(8,128)}) %reduce-scatter.6.cloned.1.call-update) | async-done | bytes 262160 | tf_op jit(solution)/shard_map/reduce_scatter | solution.py:27
  268.2 1.8 broadcast_multiply_fusion
  270.0 0.0 reduce-scatter.8.cloned.1.call-update
  270.1 6.7 %reduce-scatter.8.cloned.1.call-done = f32[1,256,256]{2,1,0:T(8,128)} async-done(((f32[2,256,256]{2,1,0:T(8,128)}), f32[1,256,256]{2,1,0:T(8,128)}) %reduce-scatter.8.cloned.1.call-update) | async-done | bytes 262160 | tf_op jit(solution)/shard_map/reduce_scatter | solution.py:43
  (1 shorter events, 0.0 us)
Async XLA Ops:
  6.5 147.9 %all-reduce.2.cloned.1.call-start = ((), (), s32[]{:S(2)}) async-start(), calls=%async_computation.3 | async-start | bytes 12582912 | tf_op jit(solution)/shard_map/psum | solution.py:11
  13.4 214.1 %reduce-scatter.4.cloned.1.call-start = ((), (), s32[]{:S(2)}) async-start(), calls=%async_computation.4 | async-start | bytes 7864320 | tf_op jit(solution)/shard_map/reduce_scatter | solution.py:26
  50.1 218.1 %reduce-scatter.6.cloned.1.call-start = ((), (), s32[]{:S(2)}) async-start(), calls=%async_computation.5 | async-start | bytes 1310720 | tf_op jit(solution)/shard_map/reduce_scatter | solution.py:27
  240.8 36.0 %reduce-scatter.8.cloned.1.call-start = ((), (), s32[]{:S(2)}) async-start(), calls=%async_computation.6 | async-start | bytes 786432 | tf_op jit(solution)/shard_map/reduce_scatter | solution.py:43
Sparse Core Ops, SparseCore 0:
  13.5 140.8 all-reduce.1
  157.4 70.0 reduce-scatter.3
  240.9 27.2 reduce-scatter.5
  270.3 6.4 reduce-scatter.7
where the time goes:
time: 283 us
  waiting for transfers between devices  211 us (75%)
  matrix products  49.9 us (18%)
  between operations  13.1 us (5%)
  other arithmetic  8.7 us (3%)
    psum x1, waiting for transfers between devices, broadcast(): return lax.psum(block, axis)  104 us
    reduce_scatter x1, waiting for transfers between devices, per_device(): mixed_rows = lax.psum_scatter(mixed, 'col', scatter_dimension=1, tiled=True)  73.1 us
    dot_general x1, matrix products, per_device(): jnp.dot(response, basis, precision=HIGHEST_PRECISION, preferred_element_t...  36.6 us
    reduce_scatter x1, waiting for transfers between devices, per_device(): lax.psum_scatter(lax.dot_general(panel, mixed_rows, (((0,), (0,)), ((), (...  27.3 us
    dot_general x1, matrix products, per_device(): lax.dot_general(panel, mixed_rows, (((0,), (0,)), ((), ())), precision=HI...  13.3 us
    select_n x1, other arithmetic, broadcast(): jnp.where(lax.axis_index(axis) == source, block, jnp.zeros_like(block))  6.82 us
    reduce_scatter x1, waiting for transfers between devices, per_device(): lax.psum_scatter(weights[:, None, None] * projected[None, :, :], 'tm', sc...  6.71 us
  transfers between devices with their start and end apart: 4, of which 4 were waited for; matrix products, arithmetic and copies ran while one was open for 13% of the time, Pallas kernels for 0%

commit v1 on v0

v1 whole, which is shorter than its diff:
```python
import jax
import jax.numpy as jnp
from jax import lax
from jax.experimental import pallas as pl
from jax.experimental.pallas import tpu as pltpu
from jax.sharding import PartitionSpec as P


HIGHEST_PRECISION = lax.Precision.HIGHEST
AXES = ("row", "col", "tm")
F32 = jnp.float32
THREE_PASSES = lax.Precision.HIGH


def broadcast(block, axis, source):
    block = jnp.where(lax.axis_index(axis) == source, block, jnp.zeros_like(block))
    return lax.psum(block, axis)


def cosine_weights(points, orders):
    moment = lax.axis_index("tm").astype(F32)
    return jnp.sqrt(2.0 / points) * jnp.cos(jnp.pi * (orders + 0.5) * (moment + 0.5) / points)


def general(g_occ, g_emp, basis):
    response = g_occ[0] * g_emp[0]
    rows_dev = response.shape[0]
    cols_dev = basis.shape[0]
    first_row = lax.axis_index("row") * rows_dev
    owner = first_row // cols_dev
    offset_local = first_row % cols_dev
    mine = lax.dynamic_slice_in_dim(basis, offset_local, rows_dev, 0)
    panel = broadcast(mine, "col", owner)
    mixed = jnp.dot(
        response, basis, precision=HIGHEST_PRECISION, preferred_element_type=F32
    )
    mixed_rows = lax.psum_scatter(mixed, "col", scatter_dimension=1, tiled=True)
    projected = lax.psum_scatter(
        lax.dot_general(
            panel,
            mixed_rows,
            (((0,), (0,)), ((), ())),
            precision=HIGHEST_PRECISION,
            preferred_element_type=F32,
        ),
        "row",
        scatter_dimension=0,
        tiled=True,
    )
    points = lax.axis_size("tm")
    orders = jnp.arange(points, dtype=jnp.int32).astype(F32)
    weights = cosine_weights(points, orders)
    return lax.psum_scatter(
        weights[:, None, None] * projected[None, :, :], "tm", scatter_dimension=0, tiled=True
    )


def accumulate(ref, value):
    @pl.when(pl.program_id(0) == 0)
    def _():
        ref[...] = value

    @pl.when(pl.program_id(0) > 0)
    def _():
        ref[...] += value


def mix_kernel(at_ref, occ_ref, emp_ref, basis_ref, *refs):
    response = occ_ref[...] * emp_ref[...]
    accumulate(refs[-1], jnp.dot(response, basis_ref[...], precision=THREE_PASSES, preferred_element_type=F32))


def mix(at, piece, tall, occ, emp, basis, held):
    rows, inner = occ.shape
    aux = basis.shape[1]
    deep = inner // 3
    unit = rows // 4
    source = pl.BlockSpec((tall, deep), lambda k, at: (at[piece * tall // unit] * unit // tall, k))
    return pl.pallas_call(
        mix_kernel,
        grid_spec=pltpu.PrefetchScalarGridSpec(
            num_scalar_prefetch=1,
            grid=(inner // deep,),
            in_specs=[source, source, pl.BlockSpec((deep, aux), lambda k, at: (k, 0))]
            + [pl.BlockSpec(memory_space=pl.ANY)] * len(held),
            out_specs=pl.BlockSpec((tall, aux), lambda k, at: (piece, 0)),
        ),
        out_shape=jax.ShapeDtypeStruct((rows, aux), F32),
        input_output_aliases={4: 0} if held else {},
        cost_estimate=pl.CostEstimate(
            flops=6 * tall * inner * aux,
            bytes_accessed=8 * tall * inner + 4 * basis.size + 4 * tall * aux,
            transcendentals=0,
        ),
        name="mix",
    )(at, occ, emp, basis, *held)


def project_kernel(at_ref, *refs):
    panels, mixed_ref, outs, sum_ref = refs[:4], refs[4], refs[5:-1], refs[-1]
    steps = pl.num_programs(0)
    for k in range(2):

        @pl.when(pl.program_id(0) == k)
        def _():
            panel = jnp.concatenate([ref[...] for ref in panels[2 * k : 2 * k + 2]])
            value = lax.dot_general(
                panel, mixed_ref[...], (((0,), (0,)), ((), ())), precision=THREE_PASSES, preferred_element_type=F32
            )
            if k == 0:
                sum_ref[...] = value
            else:
                sum_ref[...] += value

    @pl.when(pl.program_id(0) == steps - 1)
    def _():
        wide = outs[0].shape[1]
        for k, out in enumerate(outs):
            out[...] = sum_ref[:, pl.ds(pl.multiple_of(at_ref[4 + k] * wide, wide), wide)]


def project(at, panels, mixed):
    tall, wide = panels[0].shape
    rows, aux = mixed.shape
    panel = pl.BlockSpec((tall, wide), lambda k, at: (0, 0))
    return pl.pallas_call(
        project_kernel,
        grid_spec=pltpu.PrefetchScalarGridSpec(
            num_scalar_prefetch=1,
            grid=(2,),
            in_specs=[panel] * 4 + [pl.BlockSpec((2 * tall, aux), lambda k, at: (k, 0))],
            out_specs=[pl.BlockSpec((wide, aux // 4), lambda k, at: (0, 0))] * 4,
            scratch_shapes=[pltpu.VMEM((wide, aux), F32)],
        ),
        out_shape=[jax.ShapeDtypeStruct((wide, aux // 4), F32)] * 4,
        cost_estimate=pl.CostEstimate(
            flops=6 * wide * rows * aux,
            bytes_accessed=4 * rows * (wide + aux) + 4 * wide * aux,
            transcendentals=0,
        ),
        name="project",
    )(at, *panels, mixed)


def permute(x, pair):
    pairs = []
    sizes = [lax.axis_size(a) for a in AXES]
    for r in range(sizes[0]):
        for c in range(sizes[1]):
            for t in range(sizes[2]):
                to = pair(r, c, t)
                if to is not None:
                    pairs.append(tuple((a * sizes[1] + b) * sizes[2] + d for a, b, d in ((r, c, t), to)))
    return lax.ppermute(x, AXES, pairs)


RING = ((0, 1, 3, 2), (0, 2, 3, 1))


def along_ring(first, last):
    def pair(r, c, t):
        hop = RING[t].index(r ^ c)
        return (r, r ^ RING[t][hop + 1], t) if first <= hop <= last and hop < 3 else None

    return pair


def per_device(g_occ, g_emp, basis):
    occ, emp = g_occ[0], g_emp[0]
    row, col, core = (lax.axis_index(a) for a in AXES)
    rows, aux = basis.shape
    tall, wide = rows // 4, aux // 4
    chunks = (0, 3, 1, 2)

    quarter = [2 * core, 2 * core + 1, 2 - 2 * core, 3 - 2 * core]
    at = jnp.stack(quarter + [col ^ k for k in range(4)]).astype(jnp.int32)

    xor = row ^ col
    place = jnp.where(core == 0, jnp.where(xor == 3, 2, jnp.where(xor == 2, 3, xor)),
                      jnp.where(xor == 2, 1, jnp.where(xor == 3, 2, jnp.where(xor == 1, 3, xor))))

    def own(source, s, i):
        return lax.dynamic_slice(source, (quarter[s] * tall, chunks[i] * wide), (tall, wide))

    got = [[], []]
    for step in range(6):
        for s in range(2):
            if step == 0:
                out = own(lax.optimization_barrier(basis), s, 0)
            else:
                out = got[s][-1]
                if step < 4:
                    source, out = lax.optimization_barrier((basis, out))
                    out = jnp.where(place == 0, own(source, s, step), out)
            got[s].append(permute(out, along_ring(max(0, step - 3), min(2, step))))

    held = ()
    for piece, high in ((0, 2 * tall), (2, tall), (3, tall)):
        held = (mix(at, piece, high, occ, emp, basis, held),)
    (mixed,) = held

    def swap(x):
        return permute(x, lambda r, c, t: (r, c, 1 - t))

    sums = []
    gate = ()
    for i, j in enumerate(chunks):
        mine = []
        for s in range(2):
            source, seen, gate = lax.optimization_barrier((basis, got[s][i : i + 3], gate))
            mine.append(jnp.where(place == 0, own(source, s, i),
                                  jnp.where(place == 1, seen[0], jnp.where(place == 2, seen[1], seen[2]))))
        other = [swap(mine[s]) for s in range(2)]
        gate = tuple(other)
        parts = project(at, mine + other, mixed)
        total = parts[0]
        for k in (1, 2, 3):
            total = total + permute(parts[k], lambda r, c, t: (r, c ^ k, t))
        whole = total
        for k in (1, 2, 3):
            whole = whole + permute(total, lambda r, c, t: (j, c, t) if r ^ k == j else None)
        sums.append((j, whole))

    mine = sums[0][1]
    for j, part in sums[1:]:
        mine = jnp.where(row == j, part, mine)
    other = swap(mine)
    order = core.astype(F32)
    points = lax.axis_size("tm")

    def weight(moment):
        return jnp.sqrt(2.0 / points) * jnp.cos(jnp.pi * (order + 0.5) * (moment + 0.5) / points)

    return (weight(order) * mine + weight(1 - order) * other)[None]


def solution(mesh):
    sizes = [mesh.shape[a] for a in AXES]
    special = sizes == [4, 4, 2]

    def body(g_occ, g_emp, basis):
        fits = special and g_occ.shape[1] == basis.shape[0] and not basis.shape[0] % 128 and not basis.shape[1] % 512
        return (per_device if fits else general)(g_occ, g_emp, basis)

    return jax.shard_map(
        body,
        mesh=mesh,
        in_specs=(P("tm", "row", "col"), P("tm", "row", "col"), P("col", None)),
        out_specs=P("tm", "row", "col"),
        check_vma=False,
    )
```

time: 283 us -> 194 us (0.69)
  waiting for transfers between devices: 211 us -> 32.5 us
  starting transfers between devices: 0.31 us -> 74.8 us
  Pallas kernels: 0 us -> 60.7 us
  matrix products: 49.9 us -> 0 us
  other arithmetic: 8.7 us -> 21.5 us
  between operations: 13.1 us -> 0.68 us
    reduce_scatter x3 -> x0, waiting for transfers between devices: 107 us -> none  [the longest x1 73.1 us: per_device(): mixed_rows = lax.psum_scatter(mixed, 'col', scatter_dimension=1, tiled=True)]
    psum x1 -> x0, waiting for transfers between devices: 104 us -> none  [broadcast(): return lax.psum(block, axis)]
    ppermute x0 -> x45, starting transfers between devices: none -> 74.8 us  [permute(): return lax.ppermute(x, AXES, pairs)]
    pallas_call x0 -> x7, Pallas kernels: none -> 60.7 us  [the longest x3 32.1 us: mix(): pl.pallas_call(mix_kernel, grid_spec=pltpu.PrefetchScalarGridSpec(num_sca...]
    dot_general x2 -> x0, matrix products: 49.9 us -> none  [the longest x1 36.6 us: per_device(): jnp.dot(response, basis, precision=HIGHEST_PRECISION, preferred_element_t...]
    ppermute x0 -> x45, waiting for transfers between devices: none -> 32.5 us  [permute(): return lax.ppermute(x, AXES, pairs)]
    select_n x1 -> x15, other arithmetic: 6.82 us -> 17.6 us  [the longest x8 8.97 us: per_device(): jnp.where(place == 0, own(source, s, i), jnp.where(place == 1, seen[0], j...]
    add x0 -> x4, other arithmetic: none -> 3.21 us  [per_device(): total = total + permute(parts[k], lambda r, c, t: (r, c ^ k, t))]
  transfers between devices with their start and end apart: 4 -> 45, of which waited for: 4 -> 16; matrix products, arithmetic and copies ran while one was open for 13% -> 9% of each run, Pallas kernels for 0% -> 32%
where the time goes in v1:
time: 194 us; the launch traced here: 192 us
  starting transfers between devices  74.8 us (39%)
  Pallas kernels  60.7 us (31%)
  waiting for transfers between devices  32.5 us (17%)
  other arithmetic  21.5 us (11%)
  local copies, waits for them, and re-layouts  2.13 us (1%)
    ppermute x45, starting transfers between devices, permute(): return lax.ppermute(x, AXES, pairs)  74.8 us
    ppermute x45, waiting for transfers between devices, permute(): return lax.ppermute(x, AXES, pairs)  32.5 us
    pallas_call x3, Pallas kernels, mix(): pl.pallas_call(mix_kernel, grid_spec=pltpu.PrefetchScalarGridSpec(num_sca...  32.1 us
    pallas_call x4, Pallas kernels, project(): pl.pallas_call(project_kernel, grid_spec=pltpu.PrefetchScalarGridSpec(num...  28.6 us
    select_n x8, other arithmetic, per_device(): jnp.where(place == 0, own(source, s, i), jnp.where(place == 1, seen[0], j...  8.97 us
    select_n x6, other arithmetic, per_device(): out = jnp.where(place == 0, own(source, s, step), out)  7.06 us
  transfers between devices with their start and end apart: 45, of which 16 were waited for; matrix products, arithmetic and copies ran while one was open for 9% of the time, Pallas kernels for 32%

profile of v1, /device:TPU:0, one launch (start us, length us, event | category | flops | bytes accessed | tf_op | source)
XLA Modules:
  0.0 192.4 jit_solution(6080194720202164363)
XLA Ops:
  1.2 4.9 %collective-permute-start = (f32[384,256]{1,0:T(8,128)S(1)}, f32[384,256]{1,0:T(8,128)S(1)}, u32[]{:S(2)}, u32[]{:S(2)}) collective-permute-start(f32[384,256]{1,0:T(8,128)S(1)} %get-tuple-element.126), channel_id=1, source_target_pairs={{0,2},{1,5},{10,8},{11,15},{20,22},{21,17},{30,28},{31,27}} | collective-permute-start | bytes 1179656 | tf_op jit(solution)/shard_map/ppermute | solution.py:154
  7.4 3.9 %collective-permute-done = f32[384,256]{1,0:T(8,128)S(1)} collective-permute-done((f32[384,256]{1,0:T(8,128)S(1)}, f32[384,256]{1,0:T(8,128)S(1)}, u32[]{:S(2)}, u32[]{:S(2)}) %collective-permute-start) | collective-permute-done | bytes 393248 | tf_op jit(solution)/shard_map/ppermute | solution.py:154
  12.4 4.4 %collective-permute-start.1 = (f32[384,256]{1,0:T(8,128)S(1)}, f32[384,256]{1,0:T(8,128)S(1)}, u32[]{:S(2)}, u32[]{:S(2)}) collective-permute-start(f32[384,256]{1,0:T(8,128)S(1)} %dynamic-slice_select_fusion.5), channel_id=1, source_target_pairs={{0,2},{1,5},{2,6},{5,7},{8,12},{10,8},{11,15},{15,13},{17,19},{20,... | collective-permute-start | bytes 1179656 | tf_op jit(solution)/shard_map/ppermute | solution.py:154
  17.9 3.1 %collective-permute-start.8 = (f32[384,256]{1,0:T(8,128)S(1)}, f32[384,256]{1,0:T(8,128)S(1)}, u32[]{:S(2)}, u32[]{:S(2)}) collective-permute-start(f32[384,256]{1,0:T(8,128)S(1)} %dynamic-slice_select_fusion.2), channel_id=1, source_target_pairs={{0,2},{1,5},{2,6},{5,7},{8,12},{10,8},{11,15},{15,13},{17,19},{20,... | collective-permute-start | bytes 1179656 | tf_op jit(solution)/shard_map/ppermute | solution.py:154
  23.1 4.4 %collective-permute-start.2 = (f32[384,256]{1,0:T(8,128)S(1)}, f32[384,256]{1,0:T(8,128)S(1)}, u32[]{:S(2)}, u32[]{:S(2)}) collective-permute-start(f32[384,256]{1,0:T(8,128)S(1)} %dynamic-slice_select_fusion.4), channel_id=1, source_target_pairs={{0,2},{1,5},{2,6},{5,7},{6,4},{7,3},{8,12},{10,8},{11,15},{12,14},... | collective-permute-start | bytes 1179656 | tf_op jit(solution)/shard_map/ppermute | solution.py:154
  28.6 3.1 %collective-permute-start.9 = (f32[384,256]{1,0:T(8,128)S(1)}, f32[384,256]{1,0:T(8,128)S(1)}, u32[]{:S(2)}, u32[]{:S(2)}) collective-permute-start(f32[384,256]{1,0:T(8,128)S(1)} %dynamic-slice_select_fusion.1), channel_id=1, source_target_pairs={{0,2},{1,5},{2,6},{5,7},{6,4},{7,3},{8,12},{10,8},{11,15},{12,14},... | collective-permute-start | bytes 1179656 | tf_op jit(solution)/shard_map/ppermute | solution.py:154
  32.8 4.2 %collective-permute-done.9 = f32[384,256]{1,0:T(8,128)S(1)} collective-permute-done((f32[384,256]{1,0:T(8,128)S(1)}, f32[384,256]{1,0:T(8,128)S(1)}, u32[]{:S(2)}, u32[]{:S(2)}) %collective-permute-start.9) | collective-permute-done | bytes 393248 | tf_op jit(solution)/shard_map/ppermute | solution.py:154
  40.9 4.4 %collective-permute-start.3 = (f32[384,256]{1,0:T(8,128)S(1)}, f32[384,256]{1,0:T(8,128)S(1)}, u32[]{:S(2)}, u32[]{:S(2)}) collective-permute-start(f32[384,256]{1,0:T(8,128)S(1)} %dynamic-slice_select_fusion.3), channel_id=1, source_target_pairs={{0,2},{1,5},{2,6},{5,7},{6,4},{7,3},{8,12},{10,8},{11,15},{12,14},... | collective-permute-start | bytes 1179656 | tf_op jit(solution)/shard_map/ppermute | solution.py:154
  47.1 1.9 collective-permute-start.12
  50.6 4.3 %collective-permute-done.12 = f32[384,256]{1,0:T(8,128)S(1)} collective-permute-done((f32[384,256]{1,0:T(8,128)}, f32[384,256]{1,0:T(8,128)S(1)}, u32[]{:S(2)}, u32[]{:S(2)}) %collective-permute-start.12) | collective-permute-done | bytes 393248 | tf_op jit(solution)/shard_map/ppermute | solution.py:154
  59.1 13.7 %mix.3.refs_0_ = f32[1536,1024]{1,0:T(8,128)} custom-call(s32[8]{0:T(128)} %stack.35.at_ref, f32[1536,1536]{1,0:T(8,128)} %bitcast.12, f32[1536,1536]{1,0:T(8,128)} %bitcast.15, f32[1536,1024]{1,0:T(8,128)} %basis_ref.5), custom_call_target="tpu_custom_call" | custom-call | flops 7247757312 | bytes 18874368 | tf_op jit(solution)/shard_map/mix/pallas_call | solution.py:79
  72.8 9.2 %mix.4.refs_0_ = f32[1536,1024]{1,0:T(8,128)} custom-call(s32[8]{0:T(128)} %stack.35.at_ref, f32[1536,1536]{1,0:T(8,128)} %bitcast.13, f32[1536,1536]{1,0:T(8,128)} %bitcast.16, f32[1536,1024]{1,0:T(8,128)} %basis_ref.5, f32[1536,1024]{1,0:T(8,128)} %mix.3.refs_0_), custom_call_target="tpu_custom_call", output_to_operand_aliasing={{}: (4, {})} | custom-call | flops 3623878656 | bytes 12582912 | tf_op jit(solution)/shard_map/mix/pallas_call | solution.py:79
  86.4 9.2 %mix.5.refs_4_ = f32[1536,1024]{1,0:T(8,128)} custom-call(s32[8]{0:T(128)} %stack.35.at_ref, f32[1536,1536]{1,0:T(8,128)} %bitcast.14, f32[1536,1536]{1,0:T(8,128)} %bitcast.17, f32[1536,1024]{1,0:T(8,128)} %basis_ref.5, f32[1536,1024]{1,0:T(8,128)} %mix.4.refs_0_), custom_call_target="tpu_custom_call", output_to_operand_aliasing={{}: (4, {})} | custom-call | flops 3623878656 | bytes 12582912 | tf_op jit(solution)/shard_map/mix/pallas_call | solution.py:79
  95.7 7.1 %project.7 = (f32[256,256]{1,0:T(8,128)}, f32[256,256]{1,0:T(8,128)}, f32[256,256]{1,0:T(8,128)}, f32[256,256]{1,0:T(8,128)}) custom-call(s32[8]{0:T(128)} %stack.35.at_ref, f32[384,256]{1,0:T(8,128)} %copy-done.1, f32[384,256]{1,0:T(8,128)} %copy-done.3, f32[384,256]{1,0:T(8,128)} %collective-permute-done.6.refs_2_, ...), custom_call_target="tpu_custom_call" | custom-call | flops 2415919104 | bytes 8912896 | tf_op jit(solution)/shard_map/project/pallas_call | solution.py:126
  102.7 9.3 %collective-permute-start.40 = (f32[256,256]{1,0:T(8,128)}, f32[256,256]{1,0:T(8,128)S(1)}, u32[]{:S(2)}, u32[]{:S(2)}) collective-permute-start(f32[256,256]{1,0:T(8,128)} %get-tuple-element.124), channel_id=1, source_target_pairs={{0,6},{1,7},{2,4},{3,5},{4,2},{5,3},{6,0},{7,1},{8,14},{9,15},{10,... | collective-permute-start | bytes 786440 | tf_op jit(solution)/shard_map/ppermute | solution.py:154
  115.6 7.1 %project.6 = (f32[256,256]{1,0:T(8,128)}, f32[256,256]{1,0:T(8,128)}, f32[256,256]{1,0:T(8,128)}, f32[256,256]{1,0:T(8,128)}) custom-call(s32[8]{0:T(128)} %stack.35.at_ref, f32[384,256]{1,0:T(8,128)} %copy-done, f32[384,256]{1,0:T(8,128)} %copy-done.2, f32[384,256]{1,0:T(8,128)} %collective-permute-done.11.refs_2_, ...), custom_call_target="tpu_custom_call" | custom-call | flops 2415919104 | bytes 8912896 | tf_op jit(solution)/shard_map/project/pallas_call | solution.py:126
  122.7 2.9 %collective-permute-start.34 = (f32[256,256]{1,0:T(8,128)}, f32[256,256]{1,0:T(8,128)S(1)}, u32[]{:S(2)}, u32[]{:S(2)}) collective-permute-start(f32[256,256]{1,0:T(8,128)} %get-tuple-element.120), channel_id=1, source_target_pairs={{0,6},{1,7},{2,4},{3,5},{4,2},{5,3},{6,0},{7,1},{8,14},{9,15},{10,... | collective-permute-start | bytes 786440 | tf_op jit(solution)/shard_map/ppermute | solution.py:154
  125.6 7.1 %project.5 = (f32[256,256]{1,0:T(8,128)}, f32[256,256]{1,0:T(8,128)}, f32[256,256]{1,0:T(8,128)}, f32[256,256]{1,0:T(8,128)}) custom-call(s32[8]{0:T(128)} %stack.35.at_ref, f32[384,256]{1,0:T(8,128)} %copy-done.4, f32[384,256]{1,0:T(8,128)} %copy-done.6, f32[384,256]{1,0:T(8,128)} %collective-permute-done.14.refs_2_, ...), custom_call_target="tpu_custom_call" | custom-call | flops 2415919104 | bytes 8912896 | tf_op jit(solution)/shard_map/project/pallas_call | solution.py:126
  133.5 2.8 %collective-permute-start.28 = (f32[256,256]{1,0:T(8,128)}, f32[256,256]{1,0:T(8,128)}, u32[]{:S(2)}, u32[]{:S(2)}) collective-permute-start(f32[256,256]{1,0:T(8,128)} %get-tuple-element.116), channel_id=1, source_target_pairs={{0,6},{1,7},{2,4},{3,5},{4,2},{5,3},{6,0},{7,1},{8,14},{9,15},{10,... | collective-permute-start | bytes 786440 | tf_op jit(solution)/shard_map/ppermute | solution.py:154
  138.2 7.3 %project.4 = (f32[256,256]{1,0:T(8,128)}, f32[256,256]{1,0:T(8,128)}, f32[256,256]{1,0:T(8,128)}, f32[256,256]{1,0:T(8,128)}) custom-call(s32[8]{0:T(128)} %stack.35.at_ref, f32[384,256]{1,0:T(8,128)} %copy-done.5, f32[384,256]{1,0:T(8,128)} %copy-done.7, f32[384,256]{1,0:T(8,128)} %collective-permute-done.18.refs_2_, f32[384,256]{1,0:T(8,128)} %copy-done.13, ...), custom_call_target="tpu_custom_call" | custom-call | flops 2415919104 | bytes 8912896 | tf_op jit(solution)/shard_map/project/pallas_call | solution.py:126
  157.9 4.3 %collective-permute-done.42 = f32[256,256]{1,0:T(8,128)S(1)} collective-permute-done((f32[256,256]{1,0:T(8,128)S(1)}, f32[256,256]{1,0:T(8,128)S(1)}, u32[]{:S(2)}, u32[]{:S(2)}) %collective-permute-start.42) | collective-permute-done | bytes 262176 | tf_op jit(solution)/shard_map/ppermute | solution.py:154
  169.5 2.1 %collective-permute-start.29 = (f32[256,256]{1,0:T(8,128)S(1)}, f32[256,256]{1,0:T(8,128)S(1)}, u32[]{:S(2)}, u32[]{:S(2)}) collective-permute-start(f32[256,256]{1,0:T(8,128)S(1)} %add_add_fusion.2), channel_id=1, source_target_pairs={{0,8},{1,9},{2,10},{3,11},{4,12},{5,13},{6,14},{7,15}} | collective-permute-start | bytes 786440 | tf_op jit(solution)/shard_map/ppermute | solution.py:154
  173.0 10.4 %collective-permute-start.24 = (f32[256,256]{1,0:T(8,128)S(1)}, f32[256,256]{1,0:T(8,128)}, u32[]{:S(2)}, u32[]{:S(2)}) collective-permute-start(f32[256,256]{1,0:T(8,128)S(1)} %add_add_fusion.3), channel_id=1, source_target_pairs={{0,16},{1,17},{2,18},{3,19},{4,20},{5,21},{6,22},{7,23}} | collective-permute-start | bytes 786440 | tf_op jit(solution)/shard_map/ppermute | solution.py:154
  184.8 3.6 %collective-permute-done.24 = f32[256,256]{1,0:T(8,128)} collective-permute-done((f32[256,256]{1,0:T(8,128)S(1)}, f32[256,256]{1,0:T(8,128)}, u32[]{:S(2)}, u32[]{:S(2)}) %collective-permute-start.24) | collective-permute-done | bytes 262176 | tf_op jit(solution)/shard_map/ppermute | solution.py:154
  (123 shorter events, 56.6 us)
Async XLA Ops:
  56.0 26.0 %collective-permute-start.11 = (f32[384,256]{1,0:T(8,128)S(1)}, f32[384,256]{1,0:T(8,128)}, u32[]{:S(2)}, u32[]{:S(2)}) collective-permute-start(f32[384,256]{1,0:T(8,128)S(1)} %select_select_fusion.5.refs_0_), channel_id=1, source_target_pairs={{0,1},{1,0},{2,3},{3,2},{4,5},{5,4},{6,7},{7,6},{8,9},{9,8},{10,11... | collective-permute-start | bytes 1179656 | tf_op jit(solution)/shard_map/ppermute | solution.py:154
  57.2 24.7 %collective-permute-start.13 = (f32[384,256]{1,0:T(8,128)S(1)}, f32[384,256]{1,0:T(8,128)}, u32[]{:S(2)}, u32[]{:S(2)}) collective-permute-start(f32[384,256]{1,0:T(8,128)S(1)} %select_select_fusion.4.refs_1_), channel_id=1, source_target_pairs={{0,1},{1,0},{2,3},{3,2},{4,5},{5,4},{6,7},{7,6},{8,9},{9,8},{10,11... | collective-permute-start | bytes 1179656 | tf_op jit(solution)/shard_map/ppermute | solution.py:154
  57.7 24.3 %collective-permute-start.4 = (f32[384,256]{1,0:T(8,128)S(1)}, f32[384,256]{1,0:T(8,128)S(1)}, u32[]{:S(2)}, u32[]{:S(2)}) collective-permute-start(f32[384,256]{1,0:T(8,128)S(1)} %collective-permute-done.3), channel_id=1, source_target_pairs={{2,6},{5,7},{6,4},{7,3},{8,12},{12,14},{13,9},{15,13},{17,19},{18,... | collective-permute-start | bytes 1179656 | tf_op jit(solution)/shard_map/ppermute | solution.py:154
  58.4 23.6 %collective-permute-start.15 = (f32[384,256]{1,0:T(8,128)S(1)}, f32[384,256]{1,0:T(8,128)S(1)}, u32[]{:S(2)}, u32[]{:S(2)}) collective-permute-start(f32[384,256]{1,0:T(8,128)S(1)} %collective-permute-done.12), channel_id=1, source_target_pairs={{2,6},{5,7},{6,4},{7,3},{8,12},{12,14},{13,9},{15,13},{17,19},{18,... | collective-permute-start | bytes 1179656 | tf_op jit(solution)/shard_map/ppermute | solution.py:154
  83.1 28.9 %collective-permute-start.14 = (f32[384,256]{1,0:T(8,128)S(1)}, f32[384,256]{1,0:T(8,128)}, u32[]{:S(2)}, u32[]{:S(2)}) collective-permute-start(f32[384,256]{1,0:T(8,128)S(1)} %select_select_fusion.3.refs_0_), channel_id=1, source_target_pairs={{0,1},{1,0},{2,3},{3,2},{4,5},{5,4},{6,7},{7,6},{8,9},{9,8},{10,11... | collective-permute-start | bytes 1179656 | tf_op jit(solution)/shard_map/ppermute | solution.py:154
  84.4 27.7 %collective-permute-start.16 = (f32[384,256]{1,0:T(8,128)S(1)}, f32[384,256]{1,0:T(8,128)}, u32[]{:S(2)}, u32[]{:S(2)}) collective-permute-start(f32[384,256]{1,0:T(8,128)S(1)} %select_select_fusion.2.refs_1_), channel_id=1, source_target_pairs={{0,1},{1,0},{2,3},{3,2},{4,5},{5,4},{6,7},{7,6},{8,9},{9,8},{10,11... | collective-permute-start | bytes 1179656 | tf_op jit(solution)/shard_map/ppermute | solution.py:154
  84.9 27.8 %collective-permute-start.5 = (f32[384,256]{1,0:T(8,128)S(1)}, f32[384,256]{1,0:T(8,128)S(1)}, u32[]{:S(2)}, u32[]{:S(2)}) collective-permute-start(f32[384,256]{1,0:T(8,128)S(1)} %collective-permute-done.4), channel_id=1, source_target_pairs={{6,4},{7,3},{12,14},{13,9},{18,16},{19,23},{24,26},{25,29}} | collective-permute-start | bytes 1179656 | tf_op jit(solution)/shard_map/ppermute | solution.py:154
  85.6 27.1 %collective-permute-start.17 = (f32[384,256]{1,0:T(8,128)S(1)}, f32[384,256]{1,0:T(8,128)S(1)}, u32[]{:S(2)}, u32[]{:S(2)}) collective-permute-start(f32[384,256]{1,0:T(8,128)S(1)} %collective-permute-done.15), channel_id=1, source_target_pairs={{6,4},{7,3},{12,14},{13,9},{18,16},{19,23},{24,26},{25,29}} | collective-permute-start | bytes 1179656 | tf_op jit(solution)/shard_map/ppermute | solution.py:154
  102.7 19.9 %collective-permute-start.40 = (f32[256,256]{1,0:T(8,128)}, f32[256,256]{1,0:T(8,128)S(1)}, u32[]{:S(2)}, u32[]{:S(2)}) collective-permute-start(f32[256,256]{1,0:T(8,128)} %get-tuple-element.124), channel_id=1, source_target_pairs={{0,6},{1,7},{2,4},{3,5},{4,2},{5,3},{6,0},{7,1},{8,14},{9,15},{10,... | collective-permute-start | bytes 786440 | tf_op jit(solution)/shard_map/ppermute | solution.py:154
  112.0 20.7 %collective-permute-start.39 = (f32[256,256]{1,0:T(8,128)}, f32[256,256]{1,0:T(8,128)S(1)}, u32[]{:S(2)}, u32[]{:S(2)}) collective-permute-start(f32[256,256]{1,0:T(8,128)} %get-tuple-element.123), channel_id=1, source_target_pairs={{0,4},{1,5},{2,6},{3,7},{4,0},{5,1},{6,2},{7,3},{8,12},{9,13},{10,... | collective-permute-start | bytes 786440 | tf_op jit(solution)/shard_map/ppermute | solution.py:154
  112.1 20.8 %collective-permute-start.38 = (f32[256,256]{1,0:T(8,128)}, f32[256,256]{1,0:T(8,128)}, u32[]{:S(2)}, u32[]{:S(2)}) collective-permute-start(f32[256,256]{1,0:T(8,128)} %get-tuple-element.122), channel_id=1, source_target_pairs={{0,2},{1,3},{2,0},{3,1},{4,6},{5,7},{6,4},{7,5},{8,10},{9,11},{10,... | collective-permute-start | bytes 786440 | tf_op jit(solution)/shard_map/ppermute | solution.py:154
  113.8 22.5 %collective-permute-start.18 = (f32[384,256]{1,0:T(8,128)S(1)}, f32[384,256]{1,0:T(8,128)}, u32[]{:S(2)}, u32[]{:S(2)}) collective-permute-start(f32[384,256]{1,0:T(8,128)S(1)} %select_select_fusion.1.refs_0_), channel_id=1, source_target_pairs={{0,1},{1,0},{2,3},{3,2},{4,5},{5,4},{6,7},{7,6},{8,9},{9,8},{10,11... | collective-permute-start | bytes 1179656 | tf_op jit(solution)/shard_map/ppermute | solution.py:154
  115.1 21.4 %collective-permute-start.19 = (f32[384,256]{1,0:T(8,128)S(1)}, f32[384,256]{1,0:T(8,128)S(1)}, u32[]{:S(2)}, u32[]{:S(2)}) collective-permute-start(f32[384,256]{1,0:T(8,128)S(1)} %select_select_fusion.refs_1_), channel_id=1, source_target_pairs={{0,1},{1,0},{2,3},{3,2},{4,5},{5,4},{6,7},{7,6},{8,9},{9,8},{10,11... | collective-permute-start | bytes 1179656 | tf_op jit(solution)/shard_map/ppermute | solution.py:154
  132.9 13.9 %collective-permute-start.32 = (f32[256,256]{1,0:T(8,128)}, f32[256,256]{1,0:T(8,128)S(1)}, u32[]{:S(2)}, u32[]{:S(2)}) collective-permute-start(f32[256,256]{1,0:T(8,128)} %get-tuple-element.118), channel_id=1, source_target_pairs={{0,2},{1,3},{2,0},{3,1},{4,6},{5,7},{6,4},{7,5},{8,10},{9,11},{10,... | collective-permute-start | bytes 786440 | tf_op jit(solution)/shard_map/ppermute | solution.py:154
  133.5 16.0 %collective-permute-start.28 = (f32[256,256]{1,0:T(8,128)}, f32[256,256]{1,0:T(8,128)}, u32[]{:S(2)}, u32[]{:S(2)}) collective-permute-start(f32[256,256]{1,0:T(8,128)} %get-tuple-element.116), channel_id=1, source_target_pairs={{0,6},{1,7},{2,4},{3,5},{4,2},{5,3},{6,0},{7,1},{8,14},{9,15},{10,... | collective-permute-start | bytes 786440 | tf_op jit(solution)/shard_map/ppermute | solution.py:154
  136.3 16.2 %collective-permute-start.27 = (f32[256,256]{1,0:T(8,128)}, f32[256,256]{1,0:T(8,128)S(1)}, u32[]{:S(2)}, u32[]{:S(2)}) collective-permute-start(f32[256,256]{1,0:T(8,128)} %get-tuple-element.115), channel_id=1, source_target_pairs={{0,4},{1,5},{2,6},{3,7},{4,0},{5,1},{6,2},{7,3},{8,12},{9,13},{10,... | collective-permute-start | bytes 786440 | tf_op jit(solution)/shard_map/ppermute | solution.py:154
  136.4 17.3 %collective-permute-start.26 = (f32[256,256]{1,0:T(8,128)}, f32[256,256]{1,0:T(8,128)}, u32[]{:S(2)}, u32[]{:S(2)}) collective-permute-start(f32[256,256]{1,0:T(8,128)} %get-tuple-element.114), channel_id=1, source_target_pairs={{0,2},{1,3},{2,0},{3,1},{4,6},{5,7},{6,4},{7,5},{8,10},{9,11},{10,... | collective-permute-start | bytes 786440 | tf_op jit(solution)/shard_map/ppermute | solution.py:154
  146.8 15.4 %collective-permute-start.42 = (f32[256,256]{1,0:T(8,128)S(1)}, f32[256,256]{1,0:T(8,128)S(1)}, u32[]{:S(2)}, u32[]{:S(2)}) collective-permute-start(f32[256,256]{1,0:T(8,128)S(1)} %add_add_fusion), channel_id=1, source_target_pairs={{16,0},{17,1},{18,2},{19,3},{20,4},{21,5},{22,6},{23,7}} | collective-permute-start | bytes 786440 | tf_op jit(solution)/shard_map/ppermute | solution.py:154
  149.5 14.0 %collective-permute-start.22 = (f32[256,256]{1,0:T(8,128)}, f32[256,256]{1,0:T(8,128)S(1)}, u32[]{:S(2)}, u32[]{:S(2)}) collective-permute-start(f32[256,256]{1,0:T(8,128)} %get-tuple-element.112), channel_id=1, source_target_pairs={{0,6},{1,7},{2,4},{3,5},{4,2},{5,3},{6,0},{7,1},{8,14},{9,15},{10,... | collective-permute-start | bytes 786440 | tf_op jit(solution)/shard_map/ppermute | solution.py:154
  165.0 18.4 %collective-permute-start.31 = (f32[256,256]{1,0:T(8,128)S(1)}, f32[256,256]{1,0:T(8,128)S(1)}, u32[]{:S(2)}, u32[]{:S(2)}) collective-permute-start(f32[256,256]{1,0:T(8,128)S(1)} %add_add_fusion.2), channel_id=1, source_target_pairs={{16,8},{17,9},{18,10},{19,11},{20,12},{21,13},{22,14},{23,15}} | collective-permute-start | bytes 786440 | tf_op jit(solution)/shard_map/ppermute | solution.py:154
  167.7 17.1 %collective-permute-start.30 = (f32[256,256]{1,0:T(8,128)S(1)}, f32[256,256]{1,0:T(8,128)S(1)}, u32[]{:S(2)}, u32[]{:S(2)}) collective-permute-start(f32[256,256]{1,0:T(8,128)S(1)} %add_add_fusion.2), channel_id=1, source_target_pairs={{24,8},{25,9},{26,10},{27,11},{28,12},{29,13},{30,14},{31,15}} | collective-permute-start | bytes 786440 | tf_op jit(solution)/shard_map/ppermute | solution.py:154
  169.5 15.4 %collective-permute-start.29 = (f32[256,256]{1,0:T(8,128)S(1)}, f32[256,256]{1,0:T(8,128)S(1)}, u32[]{:S(2)}, u32[]{:S(2)}) collective-permute-start(f32[256,256]{1,0:T(8,128)S(1)} %add_add_fusion.2), channel_id=1, source_target_pairs={{0,8},{1,9},{2,10},{3,11},{4,12},{5,13},{6,14},{7,15}} | collective-permute-start | bytes 786440 | tf_op jit(solution)/shard_map/ppermute | solution.py:154
  171.6 13.2 %collective-permute-start.25 = (f32[256,256]{1,0:T(8,128)S(1)}, f32[256,256]{1,0:T(8,128)}, u32[]{:S(2)}, u32[]{:S(2)}) collective-permute-start(f32[256,256]{1,0:T(8,128)S(1)} %add_add_fusion.3), channel_id=1, source_target_pairs={{8,16},{9,17},{10,18},{11,19},{12,20},{13,21},{14,22},{15,23}} | collective-permute-start | bytes 786440 | tf_op jit(solution)/shard_map/ppermute | solution.py:154
  173.0 15.5 %collective-permute-start.24 = (f32[256,256]{1,0:T(8,128)S(1)}, f32[256,256]{1,0:T(8,128)}, u32[]{:S(2)}, u32[]{:S(2)}) collective-permute-start(f32[256,256]{1,0:T(8,128)S(1)} %add_add_fusion.3), channel_id=1, source_target_pairs={{0,16},{1,17},{2,18},{3,19},{4,20},{5,21},{6,22},{7,23}} | collective-permute-start | bytes 786440 | tf_op jit(solution)/shard_map/ppermute | solution.py:154
  (35 other events, 420.0 us)

commit v2 on v1

v2 whole, which is shorter than its diff:
```python
import functools

import jax
import jax.numpy as jnp
from jax import lax
from jax.experimental import pallas as pl
from jax.experimental.pallas import tpu as pltpu
from jax.sharding import PartitionSpec as P


HIGHEST_PRECISION = lax.Precision.HIGHEST
AXES = ("row", "col", "tm")
F32 = jnp.float32
THREE_PASSES = lax.Precision.HIGH
MIX_VMEM = 24 << 20
PROJECT_VMEM = 20 << 20


def broadcast(block, axis, source):
    block = jnp.where(lax.axis_index(axis) == source, block, jnp.zeros_like(block))
    return lax.psum(block, axis)


def cosine_weights(points, orders):
    moment = lax.axis_index("tm").astype(F32)
    return jnp.sqrt(2.0 / points) * jnp.cos(jnp.pi * (orders + 0.5) * (moment + 0.5) / points)


def general(g_occ, g_emp, basis):
    response = g_occ[0] * g_emp[0]
    rows_dev = response.shape[0]
    cols_dev = basis.shape[0]
    first_row = lax.axis_index("row") * rows_dev
    owner = first_row // cols_dev
    offset_local = first_row % cols_dev
    mine = lax.dynamic_slice_in_dim(basis, offset_local, rows_dev, 0)
    panel = broadcast(mine, "col", owner)
    mixed = jnp.dot(
        response, basis, precision=HIGHEST_PRECISION, preferred_element_type=F32
    )
    mixed_rows = lax.psum_scatter(mixed, "col", scatter_dimension=1, tiled=True)
    projected = lax.psum_scatter(
        lax.dot_general(
            panel,
            mixed_rows,
            (((0,), (0,)), ((), ())),
            precision=HIGHEST_PRECISION,
            preferred_element_type=F32,
        ),
        "row",
        scatter_dimension=0,
        tiled=True,
    )
    points = lax.axis_size("tm")
    orders = jnp.arange(points, dtype=jnp.int32).astype(F32)
    weights = cosine_weights(points, orders)
    return lax.psum_scatter(
        weights[:, None, None] * projected[None, :, :], "tm", scatter_dimension=0, tiled=True
    )


def mix_kernel(occ_ref, emp_ref, basis_ref, mixed_ref):
    step = pl.program_id(0)
    deep = occ_ref.shape[1]
    response = occ_ref[...] * emp_ref[...]
    part = basis_ref[pl.ds(pl.multiple_of(step * deep, deep), deep), :]
    value = jnp.dot(response, part, precision=THREE_PASSES, preferred_element_type=F32)

    @pl.when(step == 0)
    def _():
        mixed_ref[...] = value

    @pl.when(step > 0)
    def _():
        mixed_ref[...] += value


def mix(piece, tall, occ, emp, basis):
    _, inner = occ.shape
    aux = basis.shape[1]
    deep = inner // 3
    source = pl.BlockSpec((tall, deep), lambda k: (piece, k))
    return pl.pallas_call(
        mix_kernel,
        grid=(inner // deep,),
        in_specs=[source, source, pl.BlockSpec(memory_space=pltpu.VMEM)],
        out_specs=pl.BlockSpec((tall, aux), lambda k: (0, 0)),
        out_shape=jax.ShapeDtypeStruct((tall, aux), F32),
        cost_estimate=pl.CostEstimate(
            flops=6 * tall * inner * aux,
            bytes_accessed=8 * tall * inner + 4 * basis.size + 4 * tall * aux,
            transcendentals=0,
        ),
        compiler_params=pltpu.CompilerParams(vmem_limit_bytes=MIX_VMEM),
        name="mix",
    )(*(pltpu.with_memory_space_constraint(x, pltpu.HBM) for x in (occ, emp)), basis)


def project_kernel(groups, count, *refs):
    panels, mixed, outs, panel_ref, sum_ref = refs[:4], refs[4 : 4 + count], refs[4 + count : -2], refs[-2], refs[-1]
    tall = panels[0].shape[0]
    for i, ref in enumerate(panels):
        half = lax.axis_index("tm") if i < 2 else 1 - lax.axis_index("tm")
        panel_ref[pl.ds(pl.multiple_of((2 * half + i % 2) * tall, tall), tall), :] = ref[...]
    deep = mixed[0].shape[0]
    for k, ref in enumerate(mixed):
        value = lax.dot_general(
            panel_ref[k * deep : (k + 1) * deep, :],
            ref[...],
            (((0,), (0,)), ((), ())),
            precision=THREE_PASSES,
            preferred_element_type=F32,
        )
        if k == 0:
            sum_ref[...] = value
        else:
            sum_ref[...] += value
    wide = outs[0].shape[-1]

    def part(k):
        return sum_ref[:, pl.ds(pl.multiple_of((lax.axis_index("col") ^ k) * wide, wide), wide)]

    for group, out in zip(groups, outs):
        if isinstance(group, int):
            out[...] = part(group)
        else:
            for i, k in enumerate(group):
                out[i] = part(k)


def project(panels, mixed, groups):
    tall, wide = panels[0].shape
    aux = mixed[0].shape[1]
    block = (wide, aux // 4)
    whole = pl.BlockSpec(memory_space=pltpu.VMEM)
    shapes = [jax.ShapeDtypeStruct(block if isinstance(g, int) else (len(g), *block), F32) for g in groups]
    return pl.pallas_call(
        functools.partial(project_kernel, groups, len(mixed)),
        in_specs=[whole] * (4 + len(mixed)),
        out_specs=[whole] * len(shapes),
        scratch_shapes=[pltpu.VMEM((4 * tall, wide), F32), pltpu.VMEM((wide, aux), F32)],
        out_shape=shapes,
        cost_estimate=pl.CostEstimate(
            flops=24 * wide * tall * aux,
            bytes_accessed=16 * tall * (wide + aux) + 4 * wide * aux,
            transcendentals=0,
        ),
        compiler_params=pltpu.CompilerParams(vmem_limit_bytes=PROJECT_VMEM),
        name="project",
    )(*panels, *mixed)


def permute(x, pair):
    pairs = []
    sizes = [lax.axis_size(a) for a in AXES]
    for r in range(sizes[0]):
        for c in range(sizes[1]):
            for t in range(sizes[2]):
                to = pair(r, c, t)
                if to is not None:
                    pairs.append(tuple((a * sizes[1] + b) * sizes[2] + d for a, b, d in ((r, c, t), to)))
    return lax.ppermute(x, AXES, pairs)


RING = ((0, 1, 3, 2), (0, 2, 3, 1))


def along_ring(first, last):
    def pair(r, c, t):
        hop = RING[t].index(r ^ c)
        return (r, r ^ RING[t][hop + 1], t) if first <= hop <= last and hop < 3 else None

    return pair


def per_device(g_occ, g_emp, basis):
    occ, emp = g_occ[0], g_emp[0]
    row, col, core = (lax.axis_index(a) for a in AXES)
    rows, aux = basis.shape
    tall, wide = rows // 4, aux // 4
    chunks = (0, 3, 1, 2)

    quarter = [2 * core, 2 * core + 1, 2 - 2 * core, 3 - 2 * core]

    xor = row ^ col
    place = jnp.where(core == 0, jnp.where(xor == 3, 2, jnp.where(xor == 2, 3, xor)),
                      jnp.where(xor == 2, 1, jnp.where(xor == 3, 2, jnp.where(xor == 1, 3, xor))))

    def own(source, s, i):
        return lax.dynamic_slice(source, (quarter[s] * tall, chunks[i] * wide), (tall, wide))

    got = [[], []]
    for step in range(6):
        for s in range(2):
            if step == 0:
                out = own(lax.optimization_barrier(basis), s, 0)
            else:
                out = got[s][-1]
                if step < 4:
                    source, out = lax.optimization_barrier((basis, out))
                    out = jnp.where(place == 0, own(source, s, step), out)
            got[s].append(permute(out, along_ring(max(0, step - 3), min(2, step))))

    mixed = []
    for piece in range(3):
        mixed.append(mix(piece, rows // 3, occ, emp, basis))

    def swap(x):
        return permute(x, lambda r, c, t: (r, c, 1 - t))

    sums, wholes = [], []
    gate = ()
    for i, j in enumerate(chunks):
        source, seen, gate = lax.optimization_barrier((basis, [got[s][i : i + 3] for s in range(2)], gate))
        mine = [
            jnp.where(place == 0, own(source, s, i),
                      jnp.where(place == 1, seen[s][0], jnp.where(place == 2, seen[s][1], seen[s][2])))
            for s in range(2)
        ]
        other = [swap(mine[s]) for s in range(2)]
        gate = tuple(other)
        parts = project(mine + other, mixed, ((0, 2), (1, 3)) if i in (0, 2) else ((0, 1), (2, 3)) if i == 1 else (0, 1, 2, 3))
        if i < len(chunks) - 1:
            first, second = (1, 2) if i % 2 == 0 else (2, 1)
            near = parts[0] + permute(parts[1], lambda r, c, t: (r, c ^ first, t))
            total = near[0] + permute(near[1], lambda r, c, t: (r, c ^ second, t))
        else:
            total = parts[0]
            for k in (1, 2, 3):
                total = total + permute(parts[k], lambda r, c, t: (r, c ^ k, t))
        sums.append(total)
        if i % 2:
            here = chunks[i - 1]
            pair = sums[-2:]

            def pick(k):
                return jnp.where(row ^ k == here, pair[0], pair[1])

            whole = pick(0)
            for k in (1, 2, 3):
                whole = whole + permute(
                    pick(k), lambda r, c, t: (r ^ k, c, t) if r ^ k in chunks[i - 1 : i + 1] else None
                )
            wholes.append(whole)

    mine = jnp.where((row == chunks[0]) | (row == chunks[1]), wholes[0], wholes[1])
    other = swap(mine)
    order = core.astype(F32)
    points = lax.axis_size("tm")

    def weight(moment):
        return jnp.sqrt(2.0 / points) * jnp.cos(jnp.pi * (order + 0.5) * (moment + 0.5) / points)

    return (weight(order) * mine + weight(1 - order) * other)[None]


def solution(mesh):
    sizes = [mesh.shape[a] for a in AXES]
    special = sizes == [4, 4, 2]

    def body(g_occ, g_emp, basis):
        fits = special and g_occ.shape[1] == basis.shape[0] and not basis.shape[0] % 384 and not basis.shape[1] % 512
        return (per_device if fits else general)(g_occ, g_emp, basis)

    return jax.shard_map(
        body,
        mesh=mesh,
        in_specs=(P("tm", "row", "col"), P("tm", "row", "col"), P("col", None)),
        out_specs=P("tm", "row", "col"),
        check_vma=False,
    )
```

time: 194 us -> 148 us (0.76)
  Pallas kernels: 60.7 us -> 37.6 us
  waiting for transfers between devices: 32.5 us -> 18.9 us
  starting transfers between devices: 74.8 us -> 66 us
  other arithmetic: 21.5 us -> 12.9 us
  local copies, waits for them, and re-layouts: 2.13 us -> 9.99 us
    pallas_call x7, Pallas kernels: 60.7 us -> 37.6 us  [the longest x3 23 us: mix(): pl.pallas_call(mix_kernel, grid=(inner // deep,), in_specs=[source, sourc...]
    ppermute x45 -> x36, waiting for transfers between devices: 32.5 us -> 18.9 us  [permute(): return lax.ppermute(x, AXES, pairs)]
    ppermute x45 -> x36, starting transfers between devices: 74.8 us -> 66 us  [permute(): return lax.ppermute(x, AXES, pairs)]
    unnamed x28 -> x42, local copies, waits for them, and re-layouts: 0.28 us -> 8.77 us
    select_n x9, other arithmetic: 10.5 us -> 6.43 us  [the longest x4 4.61 us: per_device(): jnp.where(place == 0, own(source, s, i), jnp.where(place == 1, seen[s][0]...]
    select_n x6, other arithmetic: 7.06 us -> 4.46 us  [per_device(): out = jnp.where(place == 0, own(source, s, step), out)]
    add x4 -> x3, other arithmetic: 3.21 us -> 1.24 us  [per_device(): near = parts[0] + permute(parts[1], lambda r, c, t: (r, c ^ first, t))]
  transfers between devices with their start and end apart: 45 -> 36, of which waited for: 16 -> 10; matrix products, arithmetic and copies ran while one was open for 9% -> 8% of each run, Pallas kernels for 32% -> 26%
where the time goes in v2:
time: 148 us; the launch traced here: 146 us
  starting transfers between devices  66 us (45%)
  Pallas kernels  37.6 us (25%)
  waiting for transfers between devices  18.9 us (13%)
  other arithmetic  12.9 us (9%)
  local copies, waits for them, and re-layouts  9.99 us (7%)
    ppermute x36, starting transfers between devices, permute(): return lax.ppermute(x, AXES, pairs)  66 us
    pallas_call x3, Pallas kernels, mix(): pl.pallas_call(mix_kernel, grid=(inner // deep,), in_specs=[source, sourc...  23 us
    ppermute x36, waiting for transfers between devices, permute(): return lax.ppermute(x, AXES, pairs)  18.9 us
    pallas_call x4, Pallas kernels, project(): pl.pallas_call(functools.partial(project_kernel, groups, len(mixed)), in_...  14.5 us
    unnamed x42, local copies, waits for them, and re-layouts  8.77 us
    select_n x4, other arithmetic, per_device(): jnp.where(place == 0, own(source, s, i), jnp.where(place == 1, seen[s][0]...  4.61 us
    select_n x6, other arithmetic, per_device(): out = jnp.where(place == 0, own(source, s, step), out)  4.46 us
  transfers between devices with their start and end apart: 36, of which 10 were waited for; matrix products, arithmetic and copies ran while one was open for 8% of the time, Pallas kernels for 26%

profile of v2, /device:TPU:0, one launch (start us, length us, event | category | flops | bytes accessed | tf_op | source)
XLA Modules:
  0.0 146.3 jit_solution(4228457876654828634)
XLA Ops:
  1.2 4.9 %collective-permute-start.3 = (f32[384,256]{1,0:T(8,128)S(1)}, f32[384,256]{1,0:T(8,128)S(1)}, u32[]{:S(2)}, u32[]{:S(2)}) collective-permute-start(f32[384,256]{1,0:T(8,128)S(1)} %get-tuple-element.119), channel_id=1, source_target_pairs={{0,2},{1,5},{10,8},{11,15},{20,22},{21,17},{30,28},{31,27}} | collective-permute-start | bytes 1179656 | tf_op jit(solution)/shard_map/ppermute | solution.py:162
  7.4 3.9 %collective-permute-done.3 = f32[384,256]{1,0:T(8,128)S(1)} collective-permute-done((f32[384,256]{1,0:T(8,128)S(1)}, f32[384,256]{1,0:T(8,128)S(1)}, u32[]{:S(2)}, u32[]{:S(2)}) %collective-permute-start.3) | collective-permute-done | bytes 393248 | tf_op jit(solution)/shard_map/ppermute | solution.py:162
  12.4 4.4 %collective-permute-start.4 = (f32[384,256]{1,0:T(8,128)S(1)}, f32[384,256]{1,0:T(8,128)S(1)}, u32[]{:S(2)}, u32[]{:S(2)}) collective-permute-start(f32[384,256]{1,0:T(8,128)S(1)} %dynamic-slice_select_fusion.3), channel_id=1, source_target_pairs={{0,2},{1,5},{2,6},{5,7},{8,12},{10,8},{11,15},{15,13},{17,19},{20,... | collective-permute-start | bytes 1179656 | tf_op jit(solution)/shard_map/ppermute | solution.py:162
  18.6 3.1 %collective-permute-start.1 = (f32[384,256]{1,0:T(8,128)S(1)}, f32[384,256]{1,0:T(8,128)S(1)}, u32[]{:S(2)}, u32[]{:S(2)}) collective-permute-start(f32[384,256]{1,0:T(8,128)S(1)} %dynamic-slice_select_fusion.5), channel_id=1, source_target_pairs={{0,2},{1,5},{2,6},{5,7},{8,12},{10,8},{11,15},{15,13},{17,19},{20,... | collective-permute-start | bytes 1179656 | tf_op jit(solution)/shard_map/ppermute | solution.py:162
  23.1 4.4 %collective-permute-start.5 = (f32[384,256]{1,0:T(8,128)S(1)}, f32[384,256]{1,0:T(8,128)S(1)}, u32[]{:S(2)}, u32[]{:S(2)}) collective-permute-start(f32[384,256]{1,0:T(8,128)S(1)} %dynamic-slice_select_fusion.2), channel_id=1, source_target_pairs={{0,2},{1,5},{2,6},{5,7},{6,4},{7,3},{8,12},{10,8},{11,15},{12,14},... | collective-permute-start | bytes 1179656 | tf_op jit(solution)/shard_map/ppermute | solution.py:162
  28.7 3.9 %collective-permute-start.2 = (f32[384,256]{1,0:T(8,128)S(1)}, f32[384,256]{1,0:T(8,128)S(1)}, u32[]{:S(2)}, u32[]{:S(2)}) collective-permute-start(f32[384,256]{1,0:T(8,128)S(1)} %dynamic-slice_select_fusion.4), channel_id=1, source_target_pairs={{0,2},{1,5},{2,6},{5,7},{6,4},{7,3},{8,12},{10,8},{11,15},{12,14},... | collective-permute-start | bytes 1179656 | tf_op jit(solution)/shard_map/ppermute | solution.py:162
  32.7 2.8 %copy-done = f32[1536,1024]{1,0:T(8,128)S(1)} copy-done((f32[1536,1024]{1,0:T(8,128)S(1)}, f32[1536,1024]{1,0:T(8,128)}, u32[]{:S(2)}) %copy-start) | copy-done | bytes 6291480
  35.4 7.7 %mix.3.refs_4_ = f32[512,1024]{1,0:T(8,128)S(1)} custom-call(f32[1536,1536]{1,0:T(8,128)} %bitcast.25, f32[1536,1536]{1,0:T(8,128)} %bitcast.28, f32[1536,1024]{1,0:T(8,128)S(1)} %copy-done), custom_call_target="tpu_custom_call" | custom-call | flops 4831838208 | bytes 14680064 | tf_op jit(solution)/shard_map/mix/pallas_call | solution.py:83
  48.2 7.7 %mix.4.refs_5_ = f32[512,1024]{1,0:T(8,128)S(1)} custom-call(f32[1536,1536]{1,0:T(8,128)} %bitcast.26, f32[1536,1536]{1,0:T(8,128)} %bitcast.29, f32[1536,1024]{1,0:T(8,128)S(1)} %copy-done), custom_call_target="tpu_custom_call" | custom-call | flops 4831838208 | bytes 14680064 | tf_op jit(solution)/shard_map/mix/pallas_call | solution.py:83
  58.3 7.7 %mix.5.refs_6_ = f32[512,1024]{1,0:T(8,128)S(1)} custom-call(f32[1536,1536]{1,0:T(8,128)} %bitcast.27, f32[1536,1536]{1,0:T(8,128)} %bitcast.30, f32[1536,1024]{1,0:T(8,128)S(1)} %copy-done), custom_call_target="tpu_custom_call" | custom-call | flops 4831838208 | bytes 14680064 | tf_op jit(solution)/shard_map/mix/pallas_call | solution.py:83
  66.0 3.9 %project.4 = (f32[2,256,256]{2,1,0:T(8,128)S(1)}, f32[2,256,256]{2,1,0:T(8,128)}) custom-call(f32[384,256]{1,0:T(8,128)S(1)} %get-tuple-element.118.refs_0_, f32[384,256]{1,0:T(8,128)S(1)} %get-tuple-element.117.refs_1_, f32[384,256]{1,0:T(8,128)S(1)} %collective-permute-done.6.refs_2_, f32[384,256]{1,0:T(8,128)S(1)} %collective-permute-done.7.refs_3_, ...), custom_call_target="tpu_custom_call" | custom-call | flops 2415919104 | bytes 8912896 | tf_op jit(solution)/shard_map/project/pallas_call | solution.py:137
  69.9 5.6 %collective-permute-start.8 = (f32[2,256,256]{2,1,0:T(8,128)}, f32[2,256,256]{2,1,0:T(8,128)}, u32[]{:S(2)}, u32[]{:S(2)}) collective-permute-start(f32[2,256,256]{2,1,0:T(8,128)} %get-tuple-element.71), channel_id=1, source_target_pairs={{0,2},{1,3},{2,0},{3,1},{4,6},{5,7},{6,4},{7,5},{8,10},{9,11},{10,... | collective-permute-start | bytes 1572872 | tf_op jit(solution)/shard_map/ppermute | solution.py:162
  75.5 2.8 %select_select_fusion.2 = (f32[384,256]{1,0:T(8,128)}, f32[384,256]{1,0:T(8,128)}) fusion(f32[384,256]{1,0:T(8,128)S(1)} %collective-permute-done.5, f32[384,256]{1,0:T(8,128)S(1)} %collective-permute-done.11, f32[384,256]{1,0:T(8,128)S(1)} %collective-permute-done.20, f32[1536,1024]{1,0:T(8,128)} %basis_ref.5, s32[]{:T(128)S(6)} %select_n.236, pred[]{:T(512)S(6)} %eq.40, ...), kind=kLoop, calls=%fused_computation.2 | loop fusion | flops 589824 | bytes 3932171 | tf_op jit(solution)/shard_map/jit(_where)/select_n | solution.py:216
  85.7 3.1 %project.5 = (f32[2,256,256]{2,1,0:T(8,128)S(1)}, f32[2,256,256]{2,1,0:T(8,128)S(1)}) custom-call(f32[384,256]{1,0:T(8,128)S(1)} %get-tuple-element.116.refs_0_, f32[384,256]{1,0:T(8,128)S(1)} %get-tuple-element.115.refs_1_, f32[384,256]{1,0:T(8,128)S(1)} %copy-done.6, f32[384,256]{1,0:T(8,128)S(1)} %copy-done.8, f32[512,1024]{1,0:T(8,128)S(1)} %mix.3.refs_4_, ...), custom_call_target="tpu_custom_call" | custom-call | flops 2415919104 | bytes 8912896 | tf_op jit(solution)/shard_map/project/pallas_call | solution.py:137
  91.3 4.5 %project.6 = (f32[2,256,256]{2,1,0:T(8,128)S(1)}, f32[2,256,256]{2,1,0:T(8,128)S(1)}) custom-call(f32[384,256]{1,0:T(8,128)} %get-tuple-element.114.refs_0_, f32[384,256]{1,0:T(8,128)} %get-tuple-element.113.refs_1_, f32[384,256]{1,0:T(8,128)} %collective-permute-done.21.refs_2_, f32[384,256]{1,0:T(8,128)} %collective-permute-done.22.refs_3_, ...), custom_call_target="tpu_custom_call" | custom-call | flops 2415919104 | bytes 8912896 | tf_op jit(solution)/shard_map/project/pallas_call | solution.py:137
  95.8 2.7 %collective-permute-start.23 = (f32[2,256,256]{2,1,0:T(8,128)S(1)}, f32[2,256,256]{2,1,0:T(8,128)S(1)}, u32[]{:S(2)}, u32[]{:S(2)}) collective-permute-start(f32[2,256,256]{2,1,0:T(8,128)S(1)} %get-tuple-element.93), channel_id=1, source_target_pairs={{0,2},{1,3},{2,0},{3,1},{4,6},{5,7},{6,4},{7,5},{8,10},{9,11},{10,... | collective-permute-start | bytes 1572872 | tf_op jit(solution)/shard_map/ppermute | solution.py:162
  102.9 2.9 %collective-permute-start.15 = (f32[256,256]{1,0:T(8,128)S(1)}, f32[256,256]{1,0:T(8,128)S(1)}, u32[]{:S(2)}, u32[]{:S(2)}) collective-permute-start(f32[256,256]{1,0:T(8,128)S(1)} %slice_bitcast_fusion.2), channel_id=1, source_target_pairs={{0,2},{1,3},{2,0},{3,1},{4,6},{5,7},{6,4},{7,5},{8,10},{9,11},{10,... | collective-permute-start | bytes 786440 | tf_op jit(solution)/shard_map/ppermute | solution.py:162
  105.8 3.1 %project.7 = (f32[256,256]{1,0:T(8,128)S(1)}, f32[256,256]{1,0:T(8,128)S(1)}, f32[256,256]{1,0:T(8,128)S(1)}, f32[256,256]{1,0:T(8,128)S(1)}) custom-call(f32[384,256]{1,0:T(8,128)S(1)} %get-tuple-element.112.refs_0_, f32[384,256]{1,0:T(8,128)S(1)} %get-tuple-element.111.refs_1_, f32[384,256]{1,0:T(8,128)S(1)} %collective-permute-done.27.refs_2_, ...), custom_call_target="tpu_custom_call" | custom-call | flops 2415919104 | bytes 8912896 | tf_op jit(solution)/shard_map/project/pallas_call | solution.py:137
  119.0 3.5 %collective-permute-done.29 = f32[256,256]{1,0:T(8,128)S(1)} collective-permute-done((f32[256,256]{1,0:T(8,128)S(1)}, f32[256,256]{1,0:T(8,128)S(1)}, u32[]{:S(2)}, u32[]{:S(2)}) %collective-permute-start.29) | collective-permute-done | bytes 262176 | tf_op jit(solution)/shard_map/ppermute | solution.py:162
  122.5 5.6 %collective-permute-start.18 = (f32[256,256]{1,0:T(8,128)S(1)}, f32[256,256]{1,0:T(8,128)S(1)}, u32[]{:S(2)}, u32[]{:S(2)}) collective-permute-start(f32[256,256]{1,0:T(8,128)S(1)} %get-tuple-element.122), channel_id=1, source_target_pairs={{0,24},{1,25},{2,26},{3,27},{4,28},{5,29},{6,30},{7,31},{24,0},{25... | collective-permute-start | bytes 786440 | tf_op jit(solution)/shard_map/ppermute | solution.py:162
  130.3 3.2 %collective-permute-start.33 = (f32[256,256]{1,0:T(8,128)}, f32[256,256]{1,0:T(8,128)S(1)}, u32[]{:S(2)}, u32[]{:S(2)}) collective-permute-start(f32[256,256]{1,0:T(8,128)} %get-tuple-element.123), channel_id=1, source_target_pairs={{0,16},{1,17},{2,18},{3,19},{4,20},{5,21},{6,22},{7,23},{24,8},{25... | collective-permute-start | bytes 786440 | tf_op jit(solution)/shard_map/ppermute | solution.py:162
  134.3 3.8 %collective-permute-start.32 = (f32[256,256]{1,0:T(8,128)S(1)}, f32[256,256]{1,0:T(8,128)S(1)}, u32[]{:S(2)}, u32[]{:S(2)}) collective-permute-start(f32[256,256]{1,0:T(8,128)S(1)} %get-tuple-element.108), channel_id=1, source_target_pairs={{0,8},{1,9},{2,10},{3,11},{4,12},{5,13},{6,14},{7,15},{24,16},{25,... | collective-permute-start | bytes 786440 | tf_op jit(solution)/shard_map/ppermute | solution.py:162
  138.2 2.3 %collective-permute-done.33 = f32[256,256]{1,0:T(8,128)S(1)} collective-permute-done((f32[256,256]{1,0:T(8,128)}, f32[256,256]{1,0:T(8,128)S(1)}, u32[]{:S(2)}, u32[]{:S(2)}) %collective-permute-start.33) | collective-permute-done | bytes 262176 | tf_op jit(solution)/shard_map/ppermute | solution.py:162
  140.6 3.2 %collective-permute-done.32 = f32[256,256]{1,0:T(8,128)S(1)} collective-permute-done((f32[256,256]{1,0:T(8,128)S(1)}, f32[256,256]{1,0:T(8,128)S(1)}, u32[]{:S(2)}, u32[]{:S(2)}) %collective-permute-start.32) | collective-permute-done | bytes 262176 | tf_op jit(solution)/shard_map/ppermute | solution.py:162
  (120 shorter events, 44.6 us)
Async XLA Ops:
  23.1 20.0 %collective-permute-start.5 = (f32[384,256]{1,0:T(8,128)S(1)}, f32[384,256]{1,0:T(8,128)S(1)}, u32[]{:S(2)}, u32[]{:S(2)}) collective-permute-start(f32[384,256]{1,0:T(8,128)S(1)} %dynamic-slice_select_fusion.2), channel_id=1, source_target_pairs={{0,2},{1,5},{2,6},{5,7},{6,4},{7,3},{8,12},{10,8},{11,15},{12,14},... | collective-permute-start | bytes 1179656 | tf_op jit(solution)/shard_map/ppermute | solution.py:162
  28.7 14.4 %collective-permute-start.2 = (f32[384,256]{1,0:T(8,128)S(1)}, f32[384,256]{1,0:T(8,128)S(1)}, u32[]{:S(2)}, u32[]{:S(2)}) collective-permute-start(f32[384,256]{1,0:T(8,128)S(1)} %dynamic-slice_select_fusion.4), channel_id=1, source_target_pairs={{0,2},{1,5},{2,6},{5,7},{6,4},{7,3},{8,12},{10,8},{11,15},{12,14},... | collective-permute-start | bytes 1179656 | tf_op jit(solution)/shard_map/ppermute | solution.py:162
  43.4 12.4 %collective-permute-start.6 = (f32[384,256]{1,0:T(8,128)S(1)}, f32[384,256]{1,0:T(8,128)S(1)}, u32[]{:S(2)}, u32[]{:S(2)}) collective-permute-start(f32[384,256]{1,0:T(8,128)S(1)} %get-tuple-element.118.refs_0_), channel_id=1, source_target_pairs={{0,1},{1,0},{2,3},{3,2},{4,5},{5,4},{6,7},{7,6},{8,9},{9,8},{10,11... | collective-permute-start | bytes 1179656 | tf_op jit(solution)/shard_map/ppermute | solution.py:162
  43.5 12.3 %collective-permute-start.7 = (f32[384,256]{1,0:T(8,128)S(1)}, f32[384,256]{1,0:T(8,128)S(1)}, u32[]{:S(2)}, u32[]{:S(2)}) collective-permute-start(f32[384,256]{1,0:T(8,128)S(1)} %get-tuple-element.117.refs_1_), channel_id=1, source_target_pairs={{0,1},{1,0},{2,3},{3,2},{4,5},{5,4},{6,7},{7,6},{8,9},{9,8},{10,11... | collective-permute-start | bytes 1179656 | tf_op jit(solution)/shard_map/ppermute | solution.py:162
  44.1 11.8 %collective-permute-start.11 = (f32[384,256]{1,0:T(8,128)S(1)}, f32[384,256]{1,0:T(8,128)S(1)}, u32[]{:S(2)}, u32[]{:S(2)}) collective-permute-start(f32[384,256]{1,0:T(8,128)S(1)} %dynamic-slice_select_fusion), channel_id=1, source_target_pairs={{0,2},{1,5},{2,6},{5,7},{6,4},{7,3},{8,12},{10,8},{11,15},{12,14},... | collective-permute-start | bytes 1179656 | tf_op jit(solution)/shard_map/ppermute | solution.py:162
  56.2 19.3 %collective-permute-start.12 = (f32[384,256]{1,0:T(8,128)S(1)}, f32[384,256]{1,0:T(8,128)S(1)}, u32[]{:S(2)}, u32[]{:S(2)}) collective-permute-start(f32[384,256]{1,0:T(8,128)S(1)} %get-tuple-element.116.refs_0_), channel_id=1, source_target_pairs={{0,1},{1,0},{2,3},{3,2},{4,5},{5,4},{6,7},{7,6},{8,9},{9,8},{10,11... | collective-permute-start | bytes 1179656 | tf_op jit(solution)/shard_map/ppermute | solution.py:162
  56.2 19.2 %collective-permute-start.13 = (f32[384,256]{1,0:T(8,128)S(1)}, f32[384,256]{1,0:T(8,128)S(1)}, u32[]{:S(2)}, u32[]{:S(2)}) collective-permute-start(f32[384,256]{1,0:T(8,128)S(1)} %get-tuple-element.115.refs_1_), channel_id=1, source_target_pairs={{0,1},{1,0},{2,3},{3,2},{4,5},{5,4},{6,7},{7,6},{8,9},{9,8},{10,11... | collective-permute-start | bytes 1179656 | tf_op jit(solution)/shard_map/ppermute | solution.py:162
  56.7 18.7 %collective-permute-start.20 = (f32[384,256]{1,0:T(8,128)S(1)}, f32[384,256]{1,0:T(8,128)S(1)}, u32[]{:S(2)}, u32[]{:S(2)}) collective-permute-start(f32[384,256]{1,0:T(8,128)S(1)} %collective-permute-done.11), channel_id=1, source_target_pairs={{2,6},{5,7},{6,4},{7,3},{8,12},{12,14},{13,9},{15,13},{17,19},{18,... | collective-permute-start | bytes 1179656 | tf_op jit(solution)/shard_map/ppermute | solution.py:162
  57.4 18.1 %collective-permute-start.19 = (f32[384,256]{1,0:T(8,128)S(1)}, f32[384,256]{1,0:T(8,128)S(1)}, u32[]{:S(2)}, u32[]{:S(2)}) collective-permute-start(f32[384,256]{1,0:T(8,128)S(1)} %collective-permute-done.10), channel_id=1, source_target_pairs={{2,6},{5,7},{6,4},{7,3},{8,12},{12,14},{13,9},{15,13},{17,19},{18,... | collective-permute-start | bytes 1179656 | tf_op jit(solution)/shard_map/ppermute | solution.py:162
  69.9 18.9 %collective-permute-start.8 = (f32[2,256,256]{2,1,0:T(8,128)}, f32[2,256,256]{2,1,0:T(8,128)}, u32[]{:S(2)}, u32[]{:S(2)}) collective-permute-start(f32[2,256,256]{2,1,0:T(8,128)} %get-tuple-element.71), channel_id=1, source_target_pairs={{0,2},{1,3},{2,0},{3,1},{4,6},{5,7},{6,4},{7,5},{8,10},{9,11},{10,... | collective-permute-start | bytes 1572872 | tf_op jit(solution)/shard_map/ppermute | solution.py:162
  78.3 13.0 %collective-permute-start.21 = (f32[384,256]{1,0:T(8,128)}, f32[384,256]{1,0:T(8,128)}, u32[]{:S(2)}, u32[]{:S(2)}) collective-permute-start(f32[384,256]{1,0:T(8,128)} %get-tuple-element.114.refs_0_), channel_id=1, source_target_pairs={{0,1},{1,0},{2,3},{3,2},{4,5},{5,4},{6,7},{7,6},{8,9},{9,8},{10,11... | collective-permute-start | bytes 1179656 | tf_op jit(solution)/shard_map/ppermute | solution.py:162
  78.4 12.9 %collective-permute-start.22 = (f32[384,256]{1,0:T(8,128)}, f32[384,256]{1,0:T(8,128)}, u32[]{:S(2)}, u32[]{:S(2)}) collective-permute-start(f32[384,256]{1,0:T(8,128)} %get-tuple-element.113.refs_1_), channel_id=1, source_target_pairs={{0,1},{1,0},{2,3},{3,2},{4,5},{5,4},{6,7},{7,6},{8,9},{9,8},{10,11... | collective-permute-start | bytes 1179656 | tf_op jit(solution)/shard_map/ppermute | solution.py:162
  78.9 19.6 %collective-permute-start.26 = (f32[384,256]{1,0:T(8,128)}, f32[384,256]{1,0:T(8,128)S(1)}, u32[]{:S(2)}, u32[]{:S(2)}) collective-permute-start(f32[384,256]{1,0:T(8,128)} %copy-done.17), channel_id=1, source_target_pairs={{6,4},{7,3},{12,14},{13,9},{18,16},{19,23},{24,26},{25,29}} | collective-permute-start | bytes 1179656 | tf_op jit(solution)/shard_map/ppermute | solution.py:162
  79.6 18.9 %collective-permute-start.25 = (f32[384,256]{1,0:T(8,128)}, f32[384,256]{1,0:T(8,128)S(1)}, u32[]{:S(2)}, u32[]{:S(2)}) collective-permute-start(f32[384,256]{1,0:T(8,128)} %copy-done.19), channel_id=1, source_target_pairs={{6,4},{7,3},{12,14},{13,9},{18,16},{19,23},{24,26},{25,29}} | collective-permute-start | bytes 1179656 | tf_op jit(solution)/shard_map/ppermute | solution.py:162
  88.8 13.9 %collective-permute-start.14 = (f32[2,256,256]{2,1,0:T(8,128)S(1)}, f32[2,256,256]{2,1,0:T(8,128)S(1)}, u32[]{:S(2)}, u32[]{:S(2)}) collective-permute-start(f32[2,256,256]{2,1,0:T(8,128)S(1)} %get-tuple-element.84), channel_id=1, source_target_pairs={{0,4},{1,5},{2,6},{3,7},{4,0},{5,1},{6,2},{7,3},{8,12},{9,13},{10,... | collective-permute-start | bytes 1572872 | tf_op jit(solution)/shard_map/ppermute | solution.py:162
  95.8 15.5 %collective-permute-start.23 = (f32[2,256,256]{2,1,0:T(8,128)S(1)}, f32[2,256,256]{2,1,0:T(8,128)S(1)}, u32[]{:S(2)}, u32[]{:S(2)}) collective-permute-start(f32[2,256,256]{2,1,0:T(8,128)S(1)} %get-tuple-element.93), channel_id=1, source_target_pairs={{0,2},{1,3},{2,0},{3,1},{4,6},{5,7},{6,4},{7,5},{8,10},{9,11},{10,... | collective-permute-start | bytes 1572872 | tf_op jit(solution)/shard_map/ppermute | solution.py:162
  100.5 12.5 %collective-permute-start.9 = (f32[256,256]{1,0:T(8,128)S(1)}, f32[256,256]{1,0:T(8,128)S(1)}, u32[]{:S(2)}, u32[]{:S(2)}) collective-permute-start(f32[256,256]{1,0:T(8,128)S(1)} %slice_bitcast_fusion.4), channel_id=1, source_target_pairs={{0,4},{1,5},{2,6},{3,7},{4,0},{5,1},{6,2},{7,3},{8,12},{9,13},{10,... | collective-permute-start | bytes 786440 | tf_op jit(solution)/shard_map/ppermute | solution.py:162
  102.9 14.1 %collective-permute-start.15 = (f32[256,256]{1,0:T(8,128)S(1)}, f32[256,256]{1,0:T(8,128)S(1)}, u32[]{:S(2)}, u32[]{:S(2)}) collective-permute-start(f32[256,256]{1,0:T(8,128)S(1)} %slice_bitcast_fusion.2), channel_id=1, source_target_pairs={{0,2},{1,3},{2,0},{3,1},{4,6},{5,7},{6,4},{7,5},{8,10},{9,11},{10,... | collective-permute-start | bytes 786440 | tf_op jit(solution)/shard_map/ppermute | solution.py:162
  108.9 13.6 %collective-permute-start.29 = (f32[256,256]{1,0:T(8,128)S(1)}, f32[256,256]{1,0:T(8,128)S(1)}, u32[]{:S(2)}, u32[]{:S(2)}) collective-permute-start(f32[256,256]{1,0:T(8,128)S(1)} %get-tuple-element.102), channel_id=1, source_target_pairs={{0,2},{1,3},{2,0},{3,1},{4,6},{5,7},{6,4},{7,5},{8,10},{9,11},{10,... | collective-permute-start | bytes 786440 | tf_op jit(solution)/shard_map/ppermute | solution.py:162
  109.0 19.1 %collective-permute-start.30 = (f32[256,256]{1,0:T(8,128)S(1)}, f32[256,256]{1,0:T(8,128)S(1)}, u32[]{:S(2)}, u32[]{:S(2)}) collective-permute-start(f32[256,256]{1,0:T(8,128)S(1)} %get-tuple-element.103), channel_id=1, source_target_pairs={{0,4},{1,5},{2,6},{3,7},{4,0},{5,1},{6,2},{7,3},{8,12},{9,13},{10,... | collective-permute-start | bytes 786440 | tf_op jit(solution)/shard_map/ppermute | solution.py:162
  111.3 18.1 %collective-permute-start.31 = (f32[256,256]{1,0:T(8,128)S(1)}, f32[256,256]{1,0:T(8,128)S(1)}, u32[]{:S(2)}, u32[]{:S(2)}) collective-permute-start(f32[256,256]{1,0:T(8,128)S(1)} %get-tuple-element.104), channel_id=1, source_target_pairs={{0,6},{1,7},{2,4},{3,5},{4,2},{5,3},{6,0},{7,1},{8,14},{9,15},{10,... | collective-permute-start | bytes 786440 | tf_op jit(solution)/shard_map/ppermute | solution.py:162
  113.0 16.4 %collective-permute-start.24 = (f32[256,256]{1,0:T(8,128)S(1)}, f32[256,256]{1,0:T(8,128)S(1)}, u32[]{:S(2)}, u32[]{:S(2)}) collective-permute-start(f32[256,256]{1,0:T(8,128)S(1)} %slice_bitcast_fusion), channel_id=1, source_target_pairs={{0,4},{1,5},{2,6},{3,7},{4,0},{5,1},{6,2},{7,3},{8,12},{9,13},{10,... | collective-permute-start | bytes 786440 | tf_op jit(solution)/shard_map/ppermute | solution.py:162
  117.7 16.5 %collective-permute-start.17 = (f32[256,256]{1,0:T(8,128)S(1)}, f32[256,256]{1,0:T(8,128)S(1)}, u32[]{:S(2)}, u32[]{:S(2)}) collective-permute-start(f32[256,256]{1,0:T(8,128)S(1)} %get-tuple-element.121), channel_id=1, source_target_pairs={{8,24},{9,25},{10,26},{11,27},{12,28},{13,29},{14,30},{15,31},{16,... | collective-permute-start | bytes 786440 | tf_op jit(solution)/shard_map/ppermute | solution.py:162
  122.5 15.6 %collective-permute-start.18 = (f32[256,256]{1,0:T(8,128)S(1)}, f32[256,256]{1,0:T(8,128)S(1)}, u32[]{:S(2)}, u32[]{:S(2)}) collective-permute-start(f32[256,256]{1,0:T(8,128)S(1)} %get-tuple-element.122), channel_id=1, source_target_pairs={{0,24},{1,25},{2,26},{3,27},{4,28},{5,29},{6,30},{7,31},{24,0},{25... | collective-permute-start | bytes 786440 | tf_op jit(solution)/shard_map/ppermute | solution.py:162
  (33 other events, 253.6 us)
